TPU v7x, 256 devices: a whole 4x4x8 slice. The times are simulated.
256 devices in a mesh: ty: 16 (over y, x_hi, core), tx: 16 (over z, x_lo).
Axes of the slice: x: 4 (x_hi: 2, x_lo: 2; x = x_hi * 2 + x_lo), y: 4, z: 8, core: 2. Of those that a mesh axis runs over, the one named last changes fastest.
Arguments:
- block_input: bfloat16 [1024, 768, 256], P('ty', 'tx'), may hold values from -6 to 6
- cotangent: bfloat16 [1024, 768, 256], P('ty', 'tx'), may hold values from -6 to 6
- tissue: int32 [64, 48], P('ty', 'tx'), may hold values 0 or 1
- dw_weight: float32 [49, 256], replicated, may hold values from -0.875 to 0.875
- dw_bias: float32 [256], replicated, may hold values from -3 to 3
- ln_gain: float32 [256], replicated, may hold values from 0.5 to 1.5
- ln_bias: float32 [256], replicated, may hold values from -3 to 3
- w_expand: bfloat16 [256, 1024], replicated, may hold values from -0.375 to 0.375
- b_expand: float32 [1024], replicated, may hold values from -3 to 3
- w_reduce: bfloat16 [1024, 256], replicated, may hold values from -0.1875 to 0.1875
- layer_scale: float32 [256], replicated, may hold values from 0.5 to 2
Outputs:
- grad_input: bfloat16 [1024, 768, 256], P('ty', 'tx')
- grad_dw: float32 [49, 256], replicated
- grad_expand: float32 [256, 1024], replicated
- grad_reduce: float32 [1024, 256], replicated
Inputs may be any that keep to these rules, and one draw needn't show every extreme that they name: 1 marks a tile with tissue.
All inputs are finite; a program needn't handle non-finite values. No bound on the sum of `tissue` on one device may be relied on, other than what follows from the above.
Results may differ from a plain program's by a relative error of at most 0.007.
Values may be sent and summed in bfloat16 or wider, within the bound.
No kernel may reach another device: no remote copies, remote signals or barrier semaphores. Data moves between devices by JAX's collectives and lax.ppermute only.
A program may use at most 256 MiB of HBM per device.

v0:
```python
import math
import jax
import jax.numpy as jnp
from jax import lax
from jax.sharding import PartitionSpec as P

TILE = 16


def with_halo(block, sides, width):
    for axis, dim in sides:
        count = lax.axis_size(axis)
        forward = [(i, i + 1) for i in range(count - 1)]
        backward = [(target, source) for source, target in forward]
        low = lax.ppermute(
            lax.slice_in_dim(block, block.shape[dim] - width, None, axis=dim), axis, forward
        )
        high = lax.ppermute(lax.slice_in_dim(block, 0, width, axis=dim), axis, backward)
        block = jnp.concatenate([low, block, high], axis=dim)
    return block


def depthwise(padded, kernel, rows, cols):
    total = jnp.zeros((rows, cols, padded.shape[2]), jnp.float32)
    for row_off in range(7):
        for col_off in range(7):
            window = padded[row_off : row_off + rows, col_off : col_off + cols].astype(jnp.float32)
            total = total + window * kernel[row_off * 7 + col_off]
    return total


def filter_grad(padded, grad, rows, cols):
    gradf = grad.astype(jnp.float32)
    taps = []
    for row_off in range(7):
        for col_off in range(7):
            window = padded[row_off : row_off + rows, col_off : col_off + cols].astype(jnp.float32)
            taps.append(jnp.sum(window * gradf, axis=(0, 1)))
    return jnp.stack(taps)


def branch_back(pre, masked, ln_gain, ln_bias, w_expand, b_expand, w_reduce, layer_scale):
    center = pre - jnp.mean(pre, axis=-1, keepdims=True)
    rstd = lax.rsqrt(jnp.mean(center * center, axis=-1, keepdims=True) + 1e-06)
    nhat = center * rstd
    normed = (nhat * ln_gain + ln_bias).astype(jnp.bfloat16)
    zvals = jnp.dot(normed, w_expand, preferred_element_type=jnp.float32) + b_expand
    cdf = 0.5 * (1.0 + jax.scipy.special.erf(zvals * 0.7071067811865476))
    hidden = (zvals * cdf).astype(jnp.bfloat16)
    go_vals = (layer_scale * masked.astype(jnp.float32)).astype(jnp.bfloat16)
    dhid = jnp.dot(go_vals, w_reduce.T, preferred_element_type=jnp.float32)
    slope = cdf + zvals * jnp.exp(-0.5 * zvals * zvals) * 0.3989422804014327
    dzvals = (dhid * slope).astype(jnp.bfloat16)
    dnorm = jnp.dot(dzvals, w_expand.T, preferred_element_type=jnp.float32) * ln_gain
    grad = rstd * (
        dnorm
        - jnp.mean(dnorm, axis=-1, keepdims=True)
        - nhat * jnp.mean(dnorm * nhat, axis=-1, keepdims=True)
    )
    return (grad.astype(jnp.bfloat16), hidden, normed, go_vals, dzvals)


def body(
    block_input,
    cotangent,
    tissue,
    dw_weight,
    dw_bias,
    ln_gain,
    ln_bias,
    w_expand,
    b_expand,
    w_reduce,
    layer_scale,
):
    rows, cols, chans = block_input.shape
    mask = jnp.repeat(jnp.repeat(tissue, TILE, axis=0), TILE, axis=1)
    masked = (cotangent.astype(jnp.float32) * mask[:, :, None].astype(jnp.float32)).astype(
        jnp.bfloat16
    )
    params = (ln_gain, ln_bias, w_expand, b_expand, w_reduce, layer_scale)
    input_pad = with_halo(block_input, (("ty", 0), ("tx", 1)), 3)
    pre = depthwise(input_pad, dw_weight, rows, cols) + dw_bias
    grad, hidden, normed, go_vals, dzvals = branch_back(
        pre.reshape(-1, chans), masked.reshape(-1, chans), *params
    )
    grad_core = grad.reshape(rows, cols, chans)
    grad_pad = with_halo(grad_core, (("ty", 0), ("tx", 1)), 3)
    factor = 1.0 / math.sqrt(rows * lax.axis_size("ty") * cols * lax.axis_size("tx"))
    local_reduce = jnp.dot(hidden.T, go_vals, preferred_element_type=jnp.float32)
    local_expand = jnp.dot(normed.T, dzvals, preferred_element_type=jnp.float32)
    local_dw = filter_grad(input_pad, grad_core, rows, cols)
    total_expand, total_reduce, total_dw = lax.psum(
        (local_expand, local_reduce, local_dw), ("ty", "tx")
    )
    result = cotangent.astype(jnp.float32) + depthwise(grad_pad, dw_weight[::-1], rows, cols)
    return (
        result.astype(jnp.bfloat16),
        total_dw * factor,
        total_expand * factor,
        total_reduce * factor,
    )


def solution(mesh):
    placed = (
        P("ty", "tx", None),
        P("ty", "tx", None),
        P("ty", "tx"),
        P(),
        P(),
        P(),
        P(),
        P(),
        P(),
        P(),
        P(),
    )
    return jax.shard_map(
        body,
        mesh=mesh,
        in_specs=placed,
        out_specs=(P("ty", "tx", None), P(), P(), P()),
        check_vma=False,
    )
```

profile of v0, /device:TPU:2, one launch (start us, length us, event | category | flops | bytes accessed | tf_op | source)
XLA Modules:
  0.0 527.7 jit_solution(16179048149840862890)
XLA Ops:
  9.5 3.0 collective-permute-start
  20.4 3.8 collective-permute-start.2
  27.4 4.8 collective-permute-done.3
  32.2 61.1 %fusion.180 = (f32[64,48]{1,0:T(8,128)S(1)}, f32[64,48,256]{2,1,0:T(8,128)}) fusion(f32[256]{0:T(256)S(1)} %copy-done.23, f32[256]{0:T(256)S(1)} %bitcast.232, bf16[70,3,256]{2,1,0:T(4,128)(2,1)S(1)} %collective-permute-done.3, bf16[70,48,256]{2,1,0:T(8,128)(2,1)} %copy-done.4, f32[256]{0:T(256)S(1)} %bitcast.234, f32[256]{0:T(256)S(1)} %bitcast.140, ...), kind=kLoop, calls=%fused_computation.358 | loop fusion | flops 215479296 | bytes 16154624 | tf_op jit(solution)/shard_map/reduce_sum | solution.py:43
  93.5 2.8 multiply_reduce_fusion.1
  96.4 3.1 add_convert_fusion
  101.4 5.5 %fusion.6 = f32[1024,256]{1,0:T(8,128)} fusion(bf16[3072,256]{1,0:T(8,128)(2,1)S(1)} %copy-done.12, f32[3072,1024]{1,0:T(8,128)S(1)} %fusion.188, f32[1024]{0:T(1024)S(1)} %copy-done.27), kind=kOutput, calls=%fused_computation.99 | convolution fusion | flops 1629487104 | bytes 15208448 | tf_op jit(solution)/shard_map/dot_general | solution.py:90
  106.9 7.0 %fusion.5 = bf16[3072,1024]{1,0:T(8,128)(2,1)S(1)} fusion(f32[3072,1024]{1,0:T(8,128)S(1)} %fusion.188, bf16[3072,256]{1,0:T(8,128)(2,1)S(1)} %copy-done.12, bf16[1024,256]{1,0:T(8,128)(2,1)S(1)} %copy-done.26, f32[1024]{0:T(1024)S(1)} %copy-done.27), kind=kOutput, calls=%fused_computation.96 | convolution fusion | flops 1645215744 | bytes 20975616 | tf_op jit(solution)/shard_map/dot_general | solution.py:51
  113.9 2.7 copy-done.9
  116.5 2.8 fusion.189
  119.3 6.2 %fusion.179 = (f32[3072]{0:T(1024)S(1)}, f32[3072]{0:T(1024)S(1)}, f32[3072,256]{1,0:T(8,128)S(1)}) fusion(f32[3072]{0:T(1024)S(1)} %rsqrt.12, f32[3072]{0:T(1024)S(1)} %div.16, f32[64,48,256]{2,1,0:T(8,128)} %get-tuple-element.64, f32[256]{0:T(256)S(1)} %copy-done.25, bf16[3072,1024]{1,0:T(8,128)(2,1)} %copy-done.9, bf16[256,1024]{1,0:T(8,128)(2,1)S(1)} %copy-done), kind=kOutput, calls=%fused_computation.357 | convolution fusion | flops 1615325184 | bytes 13157376 | tf_op jit(solution)/shard_map/dot_general | solution.py:54
  125.5 2.5 multiply_convert_fusion.2
  129.4 3.8 collective-permute-start.4
  133.2 5.1 fusion.129
  138.3 6.0 %fusion.131 = (f32[256]{0:T(256)S(1)}, f32[256]{0:T(256)S(1)}, f32[256]{0:T(256)S(1)}, f32[256]{0:T(256)S(1)}, f32[256]{0:T(256)S(1)}, /*index=5*/f32[256]{0:T(2...) fusion(bf16[64,48,256]{2,1,0:T(8,128)(2,1)S(1)} %bitcast.127, bf16[70,3,256]{2,1,0:T(4,128)(2,1)S(1)} %collective-permute-done.3, ...), kind=kLoop, calls=%fused_computation.276 | loop fusion | flops 43251456 | bytes 3409920 | tf_op jit(solution)/shard_map/reduce_sum | solution.py:38
  144.3 6.4 %fusion.130 = (f32[256]{0:T(256)S(1)}, f32[256]{0:T(256)S(1)}, f32[256]{0:T(256)S(1)}, f32[256]{0:T(256)S(1)}, f32[256]{0:T(256)S(1)}, /*index=5*/f32[256]{0:T(2...) fusion(bf16[64,48,256]{2,1,0:T(8,128)(2,1)S(1)} %bitcast.128, bf16[70,3,256]{2,1,0:T(4,128)(2,1)S(1)} %collective-permute-done.3, ...), kind=kLoop, calls=%fused_computation.275 | loop fusion | flops 43251456 | bytes 3409920 | tf_op jit(solution)/shard_map/reduce_sum | solution.py:38
  150.6 5.0 fusion.126
  155.7 5.1 fusion.127
  161.7 84.7 %psum.21 = f32[49,256]{1,0:T(8,128)S(1)} all-reduce(f32[49,256]{1,0:T(8,128)S(1)} %stack.199), channel_id=1, replica_groups=mesh['ty'=16,'tx'=16] {'ty','tx'}, use_global_device_ids=true, to_apply=%region_53.0 | all-reduce | flops 12544 | bytes 100352 | tf_op jit(solution)/shard_map/psum | solution.py:93
  248.5 3.9 collective-permute-start.7
  253.1 3.9 collective-permute-done.6
  257.0 2.6 maximum_maximum_fusion
  259.6 33.2 %fusion.9 = bf16[64,48,256]{2,1,0:T(8,128)(2,1)} fusion(bf16[64,48,256]{2,1,0:T(8,128)(2,1)} %param.12, bf16[64,48,256]{2,1,0:T(8,128)(2,1)} %bitcast.134, bf16[3,48,256]{2,1,0:T(8,128)(2,1)S(1)} %collective-permute-done.5, bf16[3,48,256]{2,1,0:T(8,128)(2,1)S(1)} %collective-permute-done.4, bf16[70,51,256]{2,1,0:T(8,128)(2,1)S(1)} %get-tuple-element.66, ...), kind=kLoop, calls=%fused_computation.154 | loop fusion | flops 121896960 | bytes 70976512 | tf_op jit(solution)/shard_map/convert_element_type | solution.py:98
  292.9 223.4 %all-reduce.3.cloned.1.call-done = (f32[256,1024]{1,0:T(8,128)}, f32[1024,256]{1,0:T(8,128)}) async-done(((f32[256,1024]{1,0:T(8,128)}, f32[1024,256]{1,0:T(8,128)}), (f32[256,1024]{1,0:T(8,128)}, f32[1024,256]{1,0:T(8,128)})) %all-reduce.3.cloned.1.call-update) | async-done | bytes 2097168 | tf_op jit(solution)/shard_map/psum | solution.py:93
  (96 shorter events, 24.9 us)
Async XLA Ops:
  7.2 92.4 %copy-start = (bf16[256,1024]{1,0:T(8,128)(2,1)S(1)}, bf16[256,1024]{1,0:T(8,128)(2,1)}, u32[]{:S(2)}) copy-start(bf16[256,1024]{1,0:T(8,128)(2,1)} %param.18) | copy-start | bytes 1572868
  7.2 9.5 %copy-start.22 = (f32[256]{0:T(256)S(1)}, f32[256]{0:T(256)}, u32[]{:S(2)}) copy-start(f32[256]{0:T(256)} %param.21) | copy-start | bytes 3076
  7.2 509.0 %all-reduce.3.cloned.1.call-start = ((), (), s32[]{:S(2)}) async-start(), calls=%async_computation | async-start | bytes 4194304 | tf_op jit(solution)/shard_map/psum | solution.py:93
  8.2 10.4 %collective-permute-start.1 = (bf16[3,48,256]{2,1,0:T(8,128)(2,1)S(1)}, bf16[3,48,256]{2,1,0:T(8,128)(2,1)S(1)}, u32[]{:S(2)}, u32[]{:S(2)}) collective-permute-start(bf16[3,48,256]{2,1,0:T(8,128)(2,1)S(1)} %get-tuple-element.76), channel_id=1, source_target_pairs={{16,0},{32,16},{48,32},{64,48},{80,64},{96,80},{112,96},{128,112},... | collective-permute-start | bytes 221192 | tf_op jit(solution)/shard_map/ppermute | solution.py:18
  9.5 8.8 %collective-permute-start = (bf16[3,48,256]{2,1,0:T(8,128)(2,1)S(1)}, bf16[3,48,256]{2,1,0:T(8,128)(2,1)S(1)}, u32[]{:S(2)}, u32[]{:S(2)}) collective-permute-start(bf16[3,48,256]{2,1,0:T(8,128)(2,1)S(1)} %get-tuple-element.77), channel_id=1, source_target_pairs={{0,16},{16,32},{32,48},{48,64},{64,80},{80,96},{96,112},{112,128},... | collective-permute-start | bytes 221192 | tf_op jit(solution)/shard_map/ppermute | solution.py:15
  18.3 13.9 %copy-start.23 = (f32[256]{0:T(256)S(1)}, f32[256]{0:T(256)}, u32[]{:S(2)}) copy-start(f32[256]{0:T(256)} %param.15) | copy-start | bytes 3076
  18.7 74.6 %copy-start.2 = (bf16[67,48,256]{2,1,0:T(8,128)(2,1)}, bf16[67,48,256]{2,1,0:T(8,128)(2,1)S(1)}, u32[]{:S(2)}) copy-start(bf16[67,48,256]{2,1,0:T(8,128)(2,1)S(1)} %get-tuple-element.80) | copy-start | bytes 4939780
  20.4 7.0 %collective-permute-start.2 = (bf16[70,3,256]{2,1,0:T(4,128)(2,1)S(1)}, bf16[70,3,256]{2,1,0:T(4,128)(2,1)S(1)}, u32[]{:S(2)}, u32[]{:S(2)}) collective-permute-start(bf16[70,3,256]{2,1,0:T(4,128)(2,1)S(1)} %get-tuple-element.69), channel_id=1, source_target_pairs={{0,1},{1,2},{2,3},{3,4},{4,5},{5,6},{6,7},{7,8},{8,9},{9,10},{10,1... | collective-permute-start | bytes 322568 | tf_op jit(solution)/shard_map/ppermute | solution.py:15
  24.2 8.0 %collective-permute-start.3 = (bf16[70,3,256]{2,1,0:T(4,128)(2,1)S(1)}, bf16[70,3,256]{2,1,0:T(4,128)(2,1)S(1)}, u32[]{:S(2)}, u32[]{:S(2)}) collective-permute-start(bf16[70,3,256]{2,1,0:T(4,128)(2,1)S(1)} %get-tuple-element.70), channel_id=1, source_target_pairs={{1,0},{2,1},{3,2},{4,3},{5,4},{6,5},{7,6},{8,7},{9,8},{10,9},{11,1... | collective-permute-start | bytes 322568 | tf_op jit(solution)/shard_map/ppermute | solution.py:18
  26.2 67.1 %copy-start.14 = (f32[1,256]{1,0:T(1,128)}, f32[1,256]{1,0:T(1,128)S(1)}, u32[]{:S(2)}) copy-start(f32[1,256]{1,0:T(1,128)S(1)} %get-tuple-element.123) | copy-start | bytes 3076
  26.3 67.1 %copy-start.15 = (f32[1,256]{1,0:T(1,128)}, f32[1,256]{1,0:T(1,128)S(1)}, u32[]{:S(2)}) copy-start(f32[1,256]{1,0:T(1,128)S(1)} %get-tuple-element.124) | copy-start | bytes 3076
  26.3 67.1 %copy-start.16 = (f32[1,256]{1,0:T(1,128)}, f32[1,256]{1,0:T(1,128)S(1)}, u32[]{:S(2)}) copy-start(f32[1,256]{1,0:T(1,128)S(1)} %get-tuple-element.125) | copy-start | bytes 3076
  26.3 67.1 %copy-start.17 = (f32[1,256]{1,0:T(1,128)}, f32[1,256]{1,0:T(1,128)S(1)}, u32[]{:S(2)}) copy-start(f32[1,256]{1,0:T(1,128)S(1)} %get-tuple-element.126) | copy-start | bytes 3076
  26.3 67.1 %copy-start.18 = (f32[1,256]{1,0:T(1,128)}, f32[1,256]{1,0:T(1,128)S(1)}, u32[]{:S(2)}) copy-start(f32[1,256]{1,0:T(1,128)S(1)} %get-tuple-element.127) | copy-start | bytes 3076
  26.3 67.1 %copy-start.19 = (f32[1,256]{1,0:T(1,128)}, f32[1,256]{1,0:T(1,128)S(1)}, u32[]{:S(2)}) copy-start(f32[1,256]{1,0:T(1,128)S(1)} %get-tuple-element.128) | copy-start | bytes 3076
  26.3 67.1 %copy-start.20 = (f32[1,256]{1,0:T(1,128)}, f32[1,256]{1,0:T(1,128)S(1)}, u32[]{:S(2)}) copy-start(f32[1,256]{1,0:T(1,128)S(1)} %get-tuple-element.129) | copy-start | bytes 3076
  26.3 67.1 %copy-start.21 = (f32[1,256]{1,0:T(1,128)}, f32[1,256]{1,0:T(1,128)S(1)}, u32[]{:S(2)}) copy-start(f32[1,256]{1,0:T(1,128)S(1)} %get-tuple-element.130) | copy-start | bytes 3076
  125.5 7.6 %copy-start.5 = (bf16[70,48,256]{2,1,0:T(8,128)(2,1)S(1)}, bf16[70,48,256]{2,1,0:T(8,128)(2,1)}, u32[]{:S(2)}) copy-start(bf16[70,48,256]{2,1,0:T(8,128)(2,1)} %copy-done.4) | copy-start | bytes 5160964
  128.1 118.4 %copy-start.1 = (bf16[3072,256]{1,0:T(8,128)(2,1)}, bf16[3072,256]{1,0:T(8,128)(2,1)S(1)}, u32[]{:S(2)}) copy-start(bf16[3072,256]{1,0:T(8,128)(2,1)S(1)} %multiply_convert_fusion.2) | copy-start | bytes 4718596
  128.1 118.3 %collective-permute-start.5 = (bf16[3,48,256]{2,1,0:T(8,128)(2,1)S(1)}, bf16[3,48,256]{2,1,0:T(8,128)(2,1)S(1)}, u32[]{:S(2)}, u32[]{:S(2)}) collective-permute-start(bf16[3,48,256]{2,1,0:T(8,128)(2,1)S(1)} %bitcast.137), channel_id=1, source_target_pairs={{16,0},{32,16},{48,32},{64,48},{80,64},{96,80},{112,96},{128,112},... | collective-permute-start | bytes 221192 | tf_op jit(solution)/shard_map/ppermute | solution.py:18
  129.4 117.0 %collective-permute-start.4 = (bf16[3,48,256]{2,1,0:T(8,128)(2,1)S(1)}, bf16[3,48,256]{2,1,0:T(8,128)(2,1)S(1)}, u32[]{:S(2)}, u32[]{:S(2)}) collective-permute-start(bf16[3,48,256]{2,1,0:T(8,128)(2,1)S(1)} %bitcast.136), channel_id=1, source_target_pairs={{0,16},{16,32},{32,48},{48,64},{64,80},{80,96},{96,112},{112,128},... | collective-permute-start | bytes 221192 | tf_op jit(solution)/shard_map/ppermute | solution.py:15
  150.6 10.1 %copy-start.3 = (bf16[67,48,256]{2,1,0:T(8,128)(2,1)S(1)}, bf16[67,48,256]{2,1,0:T(8,128)(2,1)}, u32[]{:S(2)}) copy-start(bf16[67,48,256]{2,1,0:T(8,128)(2,1)} %copy-done.2) | copy-start | bytes 4939780
  246.5 10.5 %collective-permute-start.6 = (bf16[70,3,256]{2,1,0:T(4,128)(2,1)S(1)}, bf16[70,3,256]{2,1,0:T(4,128)(2,1)S(1)}, u32[]{:S(2)}, u32[]{:S(2)}) collective-permute-start(bf16[70,3,256]{2,1,0:T(4,128)(2,1)S(1)} %get-tuple-element.67), channel_id=1, source_target_pairs={{0,1},{1,2},{2,3},{3,4},{4,5},{5,6},{6,7},{7,8},{8,9},{9,10},{10,1... | collective-permute-start | bytes 322568 | tf_op jit(solution)/shard_map/ppermute | solution.py:15
  248.5 8.5 %collective-permute-start.7 = (bf16[70,3,256]{2,1,0:T(4,128)(2,1)S(1)}, bf16[70,3,256]{2,1,0:T(4,128)(2,1)S(1)}, u32[]{:S(2)}, u32[]{:S(2)}) collective-permute-start(bf16[70,3,256]{2,1,0:T(4,128)(2,1)S(1)} %get-tuple-element.68), channel_id=1, source_target_pairs={{1,0},{2,1},{3,2},{4,3},{5,4},{6,5},{7,6},{8,7},{9,8},{10,9},{11,1... | collective-permute-start | bytes 322568 | tf_op jit(solution)/shard_map/ppermute | solution.py:18
  (13 other events, 49.6 us)
Sparse Core Ops, SparseCore 0:
  253.2 262.9 all-reduce.2
where the time goes:
time: 528 us
  waiting for transfers between devices  233 us (44%)
  other arithmetic  143 us (27%)
  blocking collectives  84.7 us (16%)
  matrix products  23.2 us (4%)
  starting transfers between devices  21.1 us (4%)
  between operations  14.7 us (3%)
  local copies, waits for them, and re-layouts  7.49 us (1%)
    psum x1, waiting for transfers between devices, body(): lax.psum((local_expand, local_reduce, local_dw), ('ty', 'tx'))  223 us
    psum x1, blocking collectives, body(): lax.psum((local_expand, local_reduce, local_dw), ('ty', 'tx'))  84.7 us
    reduce_sum x1, other arithmetic, branch_back(): center = pre - jnp.mean(pre, axis=-1, keepdims=True)  61.1 us
    convert_element_type x1, other arithmetic, body(): result.astype(jnp.bfloat16)  33.2 us
    reduce_sum x6, other arithmetic, filter_grad(): taps.append(jnp.sum(window * gradf, axis=(0, 1)))  28.4 us
    ppermute x4, starting transfers between devices, with_halo(): lax.ppermute(lax.slice_in_dim(block, block.shape[dim] - width, None, axis...  12.6 us
  transfers between devices with their start and end apart: 9, of which 4 were waited for; matrix products, arithmetic and copies ran while one was open for 13% of the time, Pallas kernels for 0%

commit v1 on v0

--- a/solution.py
+++ b/solution.py
@@ -91,7 +91,7 @@
     local_expand = jnp.dot(normed.T, dzvals, preferred_element_type=jnp.float32)
     local_dw = filter_grad(input_pad, grad_core, rows, cols)
     total_expand, total_reduce, total_dw = lax.psum(
-        (local_expand, local_reduce, local_dw), ("ty", "tx")
+        lax.psum((local_expand, local_reduce, local_dw), "ty"), "tx"
     )
     result = cotangent.astype(jnp.float32) + depthwise(grad_pad, dw_weight[::-1], rows, cols)
     return (

time: 528 us -> 475 us (0.90)
  waiting for transfers between devices: 233 us -> 111 us
  blocking collectives: 84.7 us -> 131 us
  other arithmetic: 143 us -> 164 us
    psum x1 -> x2, waiting for transfers between devices: 223 us -> 101 us  [the longest x1 101 us: body(): lax.psum(lax.psum((local_expand, local_reduce, local_dw), 'ty'), 'tx')]
    psum x1 -> x2, blocking collectives: 84.7 us -> 131 us  [the longest x1 68.4 us: body(): lax.psum((local_expand, local_reduce, local_dw), 'ty')]
    convert_element_type x1, other arithmetic: 33.2 us -> 44.3 us  [body(): result.astype(jnp.bfloat16)]
    reduce_sum x6, other arithmetic: 28.4 us -> 36.8 us  [filter_grad(): taps.append(jnp.sum(window * gradf, axis=(0, 1)))]
  transfers between devices with their start and end apart: 9 -> 10, of which waited for: 4 -> 5; matrix products, arithmetic and copies ran while one was open for 13% -> 19% of each run, Pallas kernels for 0% -> 0%
where the time goes in v1:
time: 475 us; the launch traced here: 473 us
  other arithmetic  164 us (35%)
  blocking collectives  131 us (28%)
  waiting for transfers between devices  111 us (23%)
  matrix products  23.2 us (5%)
  starting transfers between devices  21.9 us (5%)
  between operations  14.5 us (3%)
  local copies, waits for them, and re-layouts  7.46 us (2%)
    psum x1, waiting for transfers between devices, body(): lax.psum(lax.psum((local_expand, local_reduce, local_dw), 'ty'), 'tx')  101 us
    psum x1, blocking collectives, body(): lax.psum((local_expand, local_reduce, local_dw), 'ty')  68.4 us
    psum x1, blocking collectives, body(): lax.psum(lax.psum((local_expand, local_reduce, local_dw), 'ty'), 'tx')  62.8 us
    reduce_sum x1, other arithmetic, branch_back(): center = pre - jnp.mean(pre, axis=-1, keepdims=True)  61 us
    convert_element_type x1, other arithmetic, body(): result.astype(jnp.bfloat16)  44.3 us
    reduce_sum x6, other arithmetic, filter_grad(): taps.append(jnp.sum(window * gradf, axis=(0, 1)))  36.8 us
    ppermute x4, starting transfers between devices, with_halo(): lax.ppermute(lax.slice_in_dim(block, block.shape[dim] - width, None, axis...  14.7 us
  transfers between devices with their start and end apart: 10, of which 5 were waited for; matrix products, arithmetic and copies ran while one was open for 19% of the time, Pallas kernels for 0%

profile of v1, /device:TPU:2, one launch (start us, length us, event | category | flops | bytes accessed | tf_op | source)
XLA Modules:
  0.0 473.3 jit_solution(13476867056003845825)
XLA Ops:
  9.5 3.0 collective-permute-start
  20.4 3.8 collective-permute-start.2
  27.4 4.8 %collective-permute-done.3 = bf16[70,3,256]{2,1,0:T(4,128)(2,1)S(1)} collective-permute-done((bf16[70,3,256]{2,1,0:T(4,128)(2,1)S(1)}, bf16[70,3,256]{2,1,0:T(4,128)(2,1)S(1)}, u32[]{:S(2)}, u32[]{:S(2)}) %collective-permute-start.3) | collective-permute-done | bytes 107552 | tf_op jit(solution)/shard_map/ppermute | solution.py:18
  32.2 61.0 %fusion.180 = (f32[64,48]{1,0:T(8,128)S(1)}, f32[64,48,256]{2,1,0:T(8,128)}) fusion(f32[256]{0:T(256)S(1)} %copy-done.15, f32[256]{0:T(256)S(1)} %bitcast.232, bf16[70,3,256]{2,1,0:T(4,128)(2,1)S(1)} %collective-permute-done.3, bf16[70,48,256]{2,1,0:T(8,128)(2,1)} %copy-done.4, f32[256]{0:T(256)S(1)} %bitcast.234, f32[256]{0:T(256)S(1)} %bitcast.140, ...), kind=kLoop, calls=%fused_computation.358 | loop fusion | flops 215479296 | bytes 16154624 | tf_op jit(solution)/shard_map/reduce_sum | solution.py:43
  93.3 2.8 multiply_reduce_fusion.1
  96.2 3.1 add_convert_fusion
  101.2 5.5 %fusion.6 = f32[1024,256]{1,0:T(8,128)} fusion(bf16[3072,256]{1,0:T(8,128)(2,1)S(1)} %copy-done.12, f32[3072,1024]{1,0:T(8,128)S(1)} %fusion.188, f32[1024]{0:T(1024)S(1)} %copy-done.19), kind=kOutput, calls=%fused_computation.99 | convolution fusion | flops 1629487104 | bytes 15208448 | tf_op jit(solution)/shard_map/dot_general | solution.py:90
  106.7 7.0 %fusion.5 = bf16[3072,1024]{1,0:T(8,128)(2,1)S(1)} fusion(f32[3072,1024]{1,0:T(8,128)S(1)} %fusion.188, bf16[3072,256]{1,0:T(8,128)(2,1)S(1)} %copy-done.12, bf16[1024,256]{1,0:T(8,128)(2,1)S(1)} %copy-done.18, f32[1024]{0:T(1024)S(1)} %copy-done.19), kind=kOutput, calls=%fused_computation.96 | convolution fusion | flops 1645215744 | bytes 20975616 | tf_op jit(solution)/shard_map/dot_general | solution.py:51
  113.6 2.7 copy-done.9
  116.3 2.8 fusion.189
  119.1 6.2 %fusion.179 = (f32[3072]{0:T(1024)S(1)}, f32[3072]{0:T(1024)S(1)}, f32[3072,256]{1,0:T(8,128)S(1)}) fusion(f32[3072]{0:T(1024)S(1)} %rsqrt.12, f32[3072]{0:T(1024)S(1)} %div.16, f32[64,48,256]{2,1,0:T(8,128)} %get-tuple-element.66, f32[256]{0:T(256)S(1)} %copy-done.17, bf16[3072,1024]{1,0:T(8,128)(2,1)} %copy-done.9, bf16[256,1024]{1,0:T(8,128)(2,1)S(1)} %copy-done), kind=kOutput, calls=%fused_computation.357 | convolution fusion | flops 1615325184 | bytes 13157376 | tf_op jit(solution)/shard_map/dot_general | solution.py:54
  130.0 3.7 collective-permute-start.4
  133.8 14.4 %fusion.131 = (f32[256]{0:T(256)S(1)}, f32[256]{0:T(256)S(1)}, f32[256]{0:T(256)S(1)}, f32[256]{0:T(256)S(1)}, f32[256]{0:T(256)S(1)}, /*index=5*/f32[256]{0:T(2...) fusion(bf16[64,48,256]{2,1,0:T(8,128)(2,1)S(1)} %bitcast.127, bf16[70,3,256]{2,1,0:T(4,128)(2,1)S(1)} %collective-permute-done.3, ...), kind=kLoop, calls=%fused_computation.276 | loop fusion | flops 43251456 | bytes 3409920 | tf_op jit(solution)/shard_map/reduce_sum | solution.py:38
  148.2 6.4 %fusion.130 = (f32[256]{0:T(256)S(1)}, f32[256]{0:T(256)S(1)}, f32[256]{0:T(256)S(1)}, f32[256]{0:T(256)S(1)}, f32[256]{0:T(256)S(1)}, /*index=5*/f32[256]{0:T(2...) fusion(bf16[64,48,256]{2,1,0:T(8,128)(2,1)S(1)} %bitcast.128, bf16[70,3,256]{2,1,0:T(4,128)(2,1)S(1)} %collective-permute-done.3, ...), kind=kLoop, calls=%fused_computation.275 | loop fusion | flops 43251456 | bytes 3409920 | tf_op jit(solution)/shard_map/reduce_sum | solution.py:38
  154.6 5.0 %fusion.126 = (f32[256]{0:T(256)S(1)}, f32[256]{0:T(256)S(1)}, f32[256]{0:T(256)S(1)}, f32[256]{0:T(256)S(1)}, f32[256]{0:T(256)S(1)}, /*index=5*/f32[256]{0:T(2...) fusion(bf16[64,48,256]{2,1,0:T(8,128)(2,1)S(1)} %bitcast.129, bf16[70,48,256]{2,1,0:T(8,128)(2,1)S(1)} %copy-done.5, ...), kind=kLoop, calls=%fused_computation.271 | loop fusion | flops 43251456 | bytes 3409920 | tf_op jit(solution)/shard_map/reduce_sum | solution.py:38
  159.6 5.1 %fusion.127 = (f32[256]{0:T(256)S(1)}, f32[256]{0:T(256)S(1)}, f32[256]{0:T(256)S(1)}, f32[256]{0:T(256)S(1)}, f32[256]{0:T(256)S(1)}, /*index=5*/f32[256]{0:T(2...) fusion(bf16[64,48,256]{2,1,0:T(8,128)(2,1)S(1)} %bitcast.130, bf16[70,48,256]{2,1,0:T(8,128)(2,1)S(1)} %copy-done.5, ...), kind=kLoop, calls=%fused_computation.272 | loop fusion | flops 43251456 | bytes 3409920 | tf_op jit(solution)/shard_map/reduce_sum | solution.py:38
  164.7 5.1 %fusion.129 = (f32[256]{0:T(256)S(1)}, f32[256]{0:T(256)S(1)}, f32[256]{0:T(256)S(1)}, f32[256]{0:T(256)S(1)}, f32[256]{0:T(256)S(1)}, /*index=5*/f32[256]{0:T(2...) fusion(bf16[64,48,256]{2,1,0:T(8,128)(2,1)S(1)} %bitcast.131, ...), kind=kLoop, calls=%fused_computation.274 | loop fusion | flops 38532608 | bytes 9809920 | tf_op jit(solution)/shard_map/reduce_sum | solution.py:38
  170.0 68.4 %psum.42 = f32[49,256]{1,0:T(8,128)S(1)} all-reduce(f32[49,256]{1,0:T(8,128)S(1)} %stack.199), channel_id=1, replica_groups=mesh['ty'=16,'tx'=16] {'ty'}, use_global_device_ids=true, to_apply=%region_53.0 | all-reduce | flops 12544 | bytes 100352 | tf_op jit(solution)/shard_map/psum | solution.py:94
  238.4 62.8 %psum.43 = f32[49,256]{1,0:T(8,128)S(1)} all-reduce(f32[49,256]{1,0:T(8,128)S(1)} %psum.42), channel_id=1, replica_groups=mesh['ty'=16,'tx'=16] {'tx'}, use_global_device_ids=true, to_apply=%region_54.0 | all-reduce | flops 12544 | bytes 100352 | tf_op jit(solution)/shard_map/psum | solution.py:93
  301.3 4.2 collective-permute-start.6
  309.1 4.2 collective-permute-done.7
  313.4 3.5 maximum_maximum_fusion
  316.9 44.3 %fusion.9 = bf16[64,48,256]{2,1,0:T(8,128)(2,1)} fusion(bf16[64,48,256]{2,1,0:T(8,128)(2,1)} %param.12, bf16[64,48,256]{2,1,0:T(8,128)(2,1)} %bitcast.134, bf16[3,48,256]{2,1,0:T(8,128)(2,1)S(1)} %collective-permute-done.5, bf16[3,48,256]{2,1,0:T(8,128)(2,1)S(1)} %collective-permute-done.4, bf16[70,51,256]{2,1,0:T(8,128)(2,1)} %get-tuple-element.68, ...), kind=kLoop, calls=%fused_computation.154 | loop fusion | flops 121896960 | bytes 70976512 | tf_op jit(solution)/shard_map/convert_element_type | solution.py:98
  361.2 100.7 %all-reduce.5.cloned.1.call-done = (f32[256,1024]{1,0:T(8,128)}, f32[1024,256]{1,0:T(8,128)}) async-done(((f32[256,1024]{1,0:T(8,128)}, f32[1024,256]{1,0:T(8,128)}), (f32[256,1024]{1,0:T(8,128)}, f32[1024,256]{1,0:T(8,128)})) %all-reduce.5.cloned.1.call-update) | async-done | bytes 2097168 | tf_op jit(solution)/shard_map/psum | solution.py:93
  (84 shorter events, 28.5 us)
Async XLA Ops:
  7.2 92.1 %copy-start = (bf16[256,1024]{1,0:T(8,128)(2,1)S(1)}, bf16[256,1024]{1,0:T(8,128)(2,1)}, u32[]{:S(2)}) copy-start(bf16[256,1024]{1,0:T(8,128)(2,1)} %param.18) | copy-start | bytes 1572868
  7.2 9.5 %copy-start.14 = (f32[256]{0:T(256)S(1)}, f32[256]{0:T(256)}, u32[]{:S(2)}) copy-start(f32[256]{0:T(256)} %param.21) | copy-start | bytes 3076
  7.2 309.7 %all-reduce.7.cloned.1.call-start = ((), (), s32[]{:S(2)}) async-start(), calls=%async_computation.1 | async-start | bytes 4194304 | tf_op jit(solution)/shard_map/psum | solution.py:94
  8.2 10.4 %collective-permute-start.1 = (bf16[3,48,256]{2,1,0:T(8,128)(2,1)S(1)}, bf16[3,48,256]{2,1,0:T(8,128)(2,1)S(1)}, u32[]{:S(2)}, u32[]{:S(2)}) collective-permute-start(bf16[3,48,256]{2,1,0:T(8,128)(2,1)S(1)} %get-tuple-element.78), channel_id=1, source_target_pairs={{16,0},{32,16},{48,32},{64,48},{80,64},{96,80},{112,96},{128,112},... | collective-permute-start | bytes 221192 | tf_op jit(solution)/shard_map/ppermute | solution.py:18
  9.5 8.8 %collective-permute-start = (bf16[3,48,256]{2,1,0:T(8,128)(2,1)S(1)}, bf16[3,48,256]{2,1,0:T(8,128)(2,1)S(1)}, u32[]{:S(2)}, u32[]{:S(2)}) collective-permute-start(bf16[3,48,256]{2,1,0:T(8,128)(2,1)S(1)} %get-tuple-element.79), channel_id=1, source_target_pairs={{0,16},{16,32},{32,48},{48,64},{64,80},{80,96},{96,112},{112,128},... | collective-permute-start | bytes 221192 | tf_op jit(solution)/shard_map/ppermute | solution.py:15
  14.6 3.6 copy-start.13
  14.6 3.7 copy-start.10
  18.3 13.9 %copy-start.15 = (f32[256]{0:T(256)S(1)}, f32[256]{0:T(256)}, u32[]{:S(2)}) copy-start(f32[256]{0:T(256)} %param.15) | copy-start | bytes 3076
  18.7 74.5 %copy-start.2 = (bf16[67,48,256]{2,1,0:T(8,128)(2,1)}, bf16[67,48,256]{2,1,0:T(8,128)(2,1)S(1)}, u32[]{:S(2)}) copy-start(bf16[67,48,256]{2,1,0:T(8,128)(2,1)S(1)} %get-tuple-element.82) | copy-start | bytes 4939780
  20.4 7.0 %collective-permute-start.2 = (bf16[70,3,256]{2,1,0:T(4,128)(2,1)S(1)}, bf16[70,3,256]{2,1,0:T(4,128)(2,1)S(1)}, u32[]{:S(2)}, u32[]{:S(2)}) collective-permute-start(bf16[70,3,256]{2,1,0:T(4,128)(2,1)S(1)} %get-tuple-element.71), channel_id=1, source_target_pairs={{0,1},{1,2},{2,3},{3,4},{4,5},{5,6},{6,7},{7,8},{8,9},{9,10},{10,1... | collective-permute-start | bytes 322568 | tf_op jit(solution)/shard_map/ppermute | solution.py:15
  24.2 8.0 %collective-permute-start.3 = (bf16[70,3,256]{2,1,0:T(4,128)(2,1)S(1)}, bf16[70,3,256]{2,1,0:T(4,128)(2,1)S(1)}, u32[]{:S(2)}, u32[]{:S(2)}) collective-permute-start(bf16[70,3,256]{2,1,0:T(4,128)(2,1)S(1)} %get-tuple-element.72), channel_id=1, source_target_pairs={{1,0},{2,1},{3,2},{4,3},{5,4},{6,5},{7,6},{8,7},{9,8},{10,9},{11,1... | collective-permute-start | bytes 322568 | tf_op jit(solution)/shard_map/ppermute | solution.py:18
  93.2 3.0 copy-start.16
  93.2 3.0 copy-start.17
  101.2 5.5 %copy-start.18 = (bf16[1024,256]{1,0:T(8,128)(2,1)S(1)}, bf16[1024,256]{1,0:T(8,128)(2,1)}, u32[]{:S(2)}) copy-start(bf16[1024,256]{1,0:T(8,128)(2,1)} %param.20) | copy-start | bytes 1572868
  119.1 6.2 %copy-start.8 = (f32[64,48,256]{2,1,0:T(8,128)S(1)}, f32[64,48,256]{2,1,0:T(8,128)}, u32[]{:S(2)}) copy-start(f32[64,48,256]{2,1,0:T(8,128)} %get-tuple-element.66) | copy-start | bytes 9437188
  127.8 173.4 %copy-start.1 = (bf16[3072,256]{1,0:T(8,128)(2,1)}, bf16[3072,256]{1,0:T(8,128)(2,1)S(1)}, u32[]{:S(2)}) copy-start(bf16[3072,256]{1,0:T(8,128)(2,1)S(1)} %multiply_convert_fusion.2) | copy-start | bytes 4718596
  128.7 172.5 %collective-permute-start.5 = (bf16[3,48,256]{2,1,0:T(8,128)(2,1)S(1)}, bf16[3,48,256]{2,1,0:T(8,128)(2,1)S(1)}, u32[]{:S(2)}, u32[]{:S(2)}) collective-permute-start(bf16[3,48,256]{2,1,0:T(8,128)(2,1)S(1)} %bitcast.137), channel_id=1, source_target_pairs={{16,0},{32,16},{48,32},{64,48},{80,64},{96,80},{112,96},{128,112},... | collective-permute-start | bytes 221192 | tf_op jit(solution)/shard_map/ppermute | solution.py:18
  130.0 171.2 %collective-permute-start.4 = (bf16[3,48,256]{2,1,0:T(8,128)(2,1)S(1)}, bf16[3,48,256]{2,1,0:T(8,128)(2,1)S(1)}, u32[]{:S(2)}, u32[]{:S(2)}) collective-permute-start(bf16[3,48,256]{2,1,0:T(8,128)(2,1)S(1)} %bitcast.136), channel_id=1, source_target_pairs={{0,16},{16,32},{32,48},{48,64},{64,80},{80,96},{96,112},{112,128},... | collective-permute-start | bytes 221192 | tf_op jit(solution)/shard_map/ppermute | solution.py:15
  133.7 328.2 %all-reduce.5.cloned.1.call-start = ((), (), s32[]{:S(2)}) async-start(), calls=%async_computation | async-start | bytes 4194304 | tf_op jit(solution)/shard_map/psum | solution.py:93
  133.7 14.4 %copy-start.5 = (bf16[70,48,256]{2,1,0:T(8,128)(2,1)S(1)}, bf16[70,48,256]{2,1,0:T(8,128)(2,1)}, u32[]{:S(2)}) copy-start(bf16[70,48,256]{2,1,0:T(8,128)(2,1)} %copy-done.4) | copy-start | bytes 5160964
  154.6 10.1 %copy-start.7 = (bf16[67,48,256]{2,1,0:T(8,128)(2,1)S(1)}, bf16[67,48,256]{2,1,0:T(8,128)(2,1)}, u32[]{:S(2)}) copy-start(bf16[67,48,256]{2,1,0:T(8,128)(2,1)} %copy-done.6) | copy-start | bytes 4939780
  154.6 10.1 %copy-start.11 = (bf16[64,48,256]{2,1,0:T(8,128)(2,1)S(1)}, bf16[64,48,256]{2,1,0:T(8,128)(2,1)}, u32[]{:S(2)}) copy-start(bf16[64,48,256]{2,1,0:T(8,128)(2,1)} %param.11) | copy-start | bytes 4718596
  301.3 7.9 %collective-permute-start.6 = (bf16[70,3,256]{2,1,0:T(4,128)(2,1)S(1)}, bf16[70,3,256]{2,1,0:T(4,128)(2,1)S(1)}, u32[]{:S(2)}, u32[]{:S(2)}) collective-permute-start(bf16[70,3,256]{2,1,0:T(4,128)(2,1)S(1)} %get-tuple-element.69), channel_id=1, source_target_pairs={{0,1},{1,2},{2,3},{3,4},{4,5},{5,6},{6,7},{7,8},{8,9},{9,10},{10,1... | collective-permute-start | bytes 322568 | tf_op jit(solution)/shard_map/ppermute | solution.py:15
  305.5 7.9 %collective-permute-start.7 = (bf16[70,3,256]{2,1,0:T(4,128)(2,1)S(1)}, bf16[70,3,256]{2,1,0:T(4,128)(2,1)S(1)}, u32[]{:S(2)}, u32[]{:S(2)}) collective-permute-start(bf16[70,3,256]{2,1,0:T(4,128)(2,1)S(1)} %get-tuple-element.70), channel_id=1, source_target_pairs={{1,0},{2,1},{3,2},{4,3},{5,4},{6,5},{7,6},{8,7},{9,8},{10,9},{11,1... | collective-permute-start | bytes 322568 | tf_op jit(solution)/shard_map/ppermute | solution.py:18
  (6 other events, 11.8 us)
Sparse Core Ops, SparseCore 0:
  133.8 158.2 all-reduce.6
  317.0 144.7 all-reduce.4
